TPU v7x, 32 devices: a whole 2x2x4 slice. The times are simulated.
32 devices in a mesh: replica: 16 (over z, y, x), dom: 2 (over core).
Axes of the slice: x: 2, y: 2, z: 4, core: 2. Of those that a mesh axis runs over, the one named last changes fastest.
Arguments:
- inputs: bfloat16 [2, 384, 8192], P(None, 'replica', 'dom'), may hold values from -6 to 6
- targets: bfloat16 [2, 384, 8192], P(None, 'replica', 'dom'), may hold values from -0.8984375 to 0.8984375
- w_first: float32 [8192, 8192], P('replica', 'dom'), may hold values from -5 to 5
- acc_first: float32 [8192, 8192], P('replica', 'dom'), may hold values from 0.5 to 8
- w_second: float32 [8192, 8192], P('dom', 'replica'), may hold values from -5 to 5
- acc_second: float32 [8192, 8192], P('dom', 'replica'), may hold values from 0.5 to 8
Outputs:
- new_first: float32 [8192, 8192], P('replica', 'dom')
- new_acc_first: float32 [8192, 8192], P('replica', 'dom')
- new_second: float32 [8192, 8192], P('dom', 'replica')
- new_acc_second: float32 [8192, 8192], P('dom', 'replica')
All inputs are finite; a program needn't handle non-finite values.
Results may differ from a plain program's by a relative error of at most 0.015.
Values may be sent and summed in bfloat16 or wider, within the bound.
No kernel may reach another device: no remote copies, remote signals or barrier semaphores. Data moves between devices by JAX's collectives and lax.ppermute only.
A program may use at most 192 MiB of HBM per device.

v0:
```python
import math
import jax
import jax.numpy as jnp
from jax import lax
from jax.sharding import PartitionSpec as P

learn_rate = 0.05
error_weight = 0.25


def local(inputs, targets, w_first, acc_first, w_second, acc_second):
    full_width = w_first.shape[1] * lax.axis_size("dom")
    unit_scale = 1.0 / math.sqrt(0.4 * full_width)
    for round_index in range(inputs.shape[0]):
        first_half = w_first.astype(jnp.bfloat16)
        second_half = w_second.astype(jnp.bfloat16)
        round_batch = lax.all_gather(inputs[round_index], "replica", axis=0, tiled=True)
        goal_rows = targets[round_index]
        first_terms = (
            lax.dot_general(
                round_batch,
                first_half,
                (((1,), (1,)), ((), ())),
                preferred_element_type=jnp.float32,
            )
            * unit_scale
        )
        first_out = jnp.tanh(lax.psum(first_terms.astype(jnp.bfloat16), "dom").astype(jnp.float32))
        first_rows = first_out.astype(jnp.bfloat16)
        second_out = jnp.tanh(
            lax.psum_scatter(
                lax.dot_general(
                    first_rows,
                    second_half,
                    (((1,), (1,)), ((), ())),
                    preferred_element_type=jnp.float32,
                )
                * unit_scale,
                "replica",
                scatter_dimension=0,
                tiled=True,
            )
        )
        error_own = (
            (second_out - goal_rows.astype(jnp.float32))
            * error_weight
            * (1.0 - second_out * second_out)
        ).astype(jnp.bfloat16)
        error_half = lax.all_gather(error_own, "replica", axis=0, tiled=True)
        second_grad = lax.dot_general(
            error_half, first_rows, (((0,), (0,)), ((), ())), preferred_element_type=jnp.float32
        )
        back_terms = (
            jnp.dot(error_half, second_half, preferred_element_type=jnp.float32) * unit_scale
        )
        back_pre = lax.psum(back_terms.astype(jnp.bfloat16), "dom").astype(jnp.float32)
        first_error = (back_pre * (1.0 - first_out * first_out)).astype(jnp.bfloat16)
        first_grad = lax.dot_general(
            first_error, round_batch, (((0,), (0,)), ((), ())), preferred_element_type=jnp.float32
        )
        acc_first = acc_first + first_grad * first_grad
        w_first = w_first - learn_rate * first_grad / jnp.sqrt(acc_first)
        acc_second = acc_second + second_grad * second_grad
        w_second = w_second - learn_rate * second_grad / jnp.sqrt(acc_second)
    return (w_first, acc_first, w_second, acc_second)


def solution(mesh):
    placed = (
        P(None, "replica", "dom"),
        P(None, "replica", "dom"),
        P("replica", "dom"),
        P("replica", "dom"),
        P("dom", "replica"),
        P("dom", "replica"),
    )
    return jax.shard_map(
        local,
        mesh=mesh,
        in_specs=placed,
        out_specs=(
            P("replica", "dom"),
            P("replica", "dom"),
            P("dom", "replica"),
            P("dom", "replica"),
        ),
        check_vma=False,
    )
```

profile of v0, /device:TPU:0, one launch (start us, length us, event | category | flops | bytes accessed | tf_op | source)
XLA Modules:
  0.0 729.3 jit_solution(1402167555871297250)
XLA Ops:
  7.2 1.8 fusion.71
  9.1 73.1 %all-gather.11.cloned.1.call-done = bf16[1,384,4096]{2,1,0:T(8,128)(2,1)} async-done(((bf16[1,24,4096]{2,1,0:T(8,128)(2,1)}), bf16[1,384,4096]{2,1,0:T(8,128)(2,1)}) %all-gather.11.cloned.1.call-update) | async-done | bytes 3145744 | tf_op jit(solution)/shard_map/all_gather | solution.py:17
  82.2 6.9 fusion.37
  89.2 17.1 %all-reduce.5.cloned.1.call-done = bf16[384,512]{1,0:T(8,128)(2,1)} async-done(((bf16[384,512]{1,0:T(8,128)(2,1)}), bf16[384,512]{1,0:T(8,128)(2,1)}) %all-reduce.5.cloned.1.call-update) | async-done | bytes 393232 | tf_op jit(solution)/shard_map/psum | solution.py:28
  106.3 8.1 %convolution_multiply_fusion.1 = f32[384,4096]{1,0:T(8,128)} fusion(f32[4096,512]{1,0:T(8,128)} %param.10, bf16[384,512]{1,0:T(8,128)(2,1)} %all-reduce.5.cloned.1.call-done), kind=kOutput, calls=%fused_computation.9 | convolution fusion | flops 1614675968 | bytes 15073280 | tf_op jit(solution)/shard_map/dot_general | solution.py:32
  114.4 147.1 %reduce-scatter.3.cloned.1.call-done = f32[24,4096]{1,0:T(8,128)} async-done(((f32[384,4096]{1,0:T(8,128)}), f32[24,4096]{1,0:T(8,128)}) %reduce-scatter.3.cloned.1.call-update) | async-done | bytes 393232 | tf_op jit(solution)/shard_map/reduce_scatter | solution.py:31
  261.5 1.8 fusion.60
  263.4 69.0 %all-gather.7.cloned.1.call-done = bf16[384,4096]{1,0:T(8,128)(2,1)} async-done(((bf16[24,4096]{1,0:T(8,128)(2,1)}), bf16[384,4096]{1,0:T(8,128)(2,1)}) %all-gather.7.cloned.1.call-update) | async-done | bytes 3145744 | tf_op jit(solution)/shard_map/all_gather | solution.py:49
  332.4 6.9 fusion.45
  339.3 0.5 all-gather.13.cloned.1.call-update
  339.9 16.5 %all-reduce.7.cloned.1.call-done = bf16[384,512]{1,0:T(8,128)(2,1)} async-done(((bf16[384,512]{1,0:T(8,128)(2,1)}), bf16[384,512]{1,0:T(8,128)(2,1)}) %all-reduce.7.cloned.1.call-update) | async-done | bytes 393232 | tf_op jit(solution)/shard_map/psum | solution.py:56
  356.4 6.8 fusion.7
  363.2 65.8 %all-gather.13.cloned.1.call-done = bf16[1,384,4096]{2,1,0:T(8,128)(2,1)} async-done(((bf16[1,24,4096]{2,1,0:T(8,128)(2,1)}), bf16[1,384,4096]{2,1,0:T(8,128)(2,1)}) %all-gather.13.cloned.1.call-update) | async-done | bytes 3145744 | tf_op jit(solution)/shard_map/all_gather | solution.py:17
  429.0 12.2 %fusion.48 = bf16[384,512]{1,0:T(8,128)(2,1)} fusion(bf16[1,384,4096]{2,1,0:T(8,128)(2,1)} %all-gather.13.cloned.1.call-done, f32[512,4096]{1,0:T(8,128)} %param.8, f32[512,4096]{1,0:T(8,128)} %fusion.7, f32[512,4096]{1,0:T(8,128)} %param.9), kind=kOutput, calls=%fused_computation.34 | convolution fusion | flops 1623588864 | bytes 28704768 | tf_op jit(solution)/shard_map/dot_general | solution.py:20
  441.4 11.2 %multiply_subtract_fusion.2 = (f32[4096,512]{1,0:T(8,128)}, f32[4096,512]{1,0:T(8,128)}) fusion(f32[4096,512]{1,0:T(8,128)} %param.10, f32[4096,512]{1,0:T(8,128)} %param.11, bf16[384,4096]{1,0:T(8,128)(2,1)S(1)} %copy-done.1, bf16[384,512]{1,0:T(8,128)(2,1)S(1)} %copy-done.4), kind=kOutput, calls=%fused_computation.4 | convolution fusion | flops 1621491712 | bytes 37093376 | tf_op jit(solution)/shard_map/dot_general | solution.py:50
  452.6 5.7 all-reduce.9.cloned.1.call-done
  458.3 8.1 %convolution_multiply_fusion = f32[384,4096]{1,0:T(8,128)} fusion(f32[4096,512]{1,0:T(8,128)} %get-tuple-element.10, bf16[384,512]{1,0:T(8,128)(2,1)} %all-reduce.9.cloned.1.call-done), kind=kOutput, calls=%fused_computation.8 | convolution fusion | flops 1614675968 | bytes 15073280 | tf_op jit(solution)/shard_map/dot_general | solution.py:32
  466.5 146.6 %reduce-scatter.5.cloned.1.call-done = f32[24,4096]{1,0:T(8,128)} async-done(((f32[384,4096]{1,0:T(8,128)}), f32[24,4096]{1,0:T(8,128)}) %reduce-scatter.5.cloned.1.call-update) | async-done | bytes 393232 | tf_op jit(solution)/shard_map/reduce_scatter | solution.py:31
  613.1 1.8 fusion.57
  615.0 69.2 %all-gather.9.cloned.1.call-done = bf16[384,4096]{1,0:T(8,128)(2,1)} async-done(((bf16[24,4096]{1,0:T(8,128)(2,1)}), bf16[384,4096]{1,0:T(8,128)(2,1)}) %all-gather.9.cloned.1.call-update) | async-done | bytes 3145744 | tf_op jit(solution)/shard_map/all_gather | solution.py:49
  684.2 6.9 fusion.42
  691.1 14.7 %multiply_subtract_fusion = (f32[4096,512]{1,0:T(8,128)}, f32[4096,512]{1,0:T(8,128)}) fusion(f32[4096,512]{1,0:T(8,128)} %get-tuple-element.10, f32[4096,512]{1,0:T(8,128)} %param.11, f32[4096,512]{1,0:T(8,128)} %get-tuple-element.11, bf16[384,4096]{1,0:T(8,128)(2,1)} %all-gather.9.cloned.1.call-done, bf16[384,512]{1,0:T(8,128)(2,1)S(1)} %copy-done.3), kind=kOutput, calls=%fused_computation | convolution fusion | flops 1625686016 | bytes 45481984 | tf_op jit(solution)/shard_map/dot_general | solution.py:50
  705.8 2.4 all-reduce.11.cloned.1.call-done
  708.2 14.2 %multiply_subtract_fusion.1 = (f32[512,4096]{1,0:T(8,128)}, f32[512,4096]{1,0:T(8,128)}) fusion(f32[512,4096]{1,0:T(8,128)} %param.8, f32[512,4096]{1,0:T(8,128)} %param.9, f32[512,4096]{1,0:T(8,128)} %fusion.7, bf16[1,384,4096]{2,1,0:T(8,128)(2,1)S(1)} %copy-done, bf16[384,512]{1,0:T(8,128)(2,1)} %all-reduce.11.cloned.1.call-done, ...), kind=kOutput, calls=%fused_computation.2 | convolution fusion | flops 1632763904 | bytes 45875200 | tf_op jit(solution)/shard_map/dot_general | solution.py:58
  (31 shorter events, 0.8 us)
Async XLA Ops:
  7.2 75.1 %all-gather.11.cloned.1.call-start = ((), (), s32[]{:S(2)}) async-start(), calls=%async_computation.10 | async-start | bytes 3342336 | tf_op jit(solution)/shard_map/all_gather | solution.py:17
  9.0 97.3 %all-reduce.5.cloned.1.call-start = ((), (), s32[]{:S(2)}) async-start(), calls=%async_computation.2 | async-start | bytes 786432 | tf_op jit(solution)/shard_map/psum | solution.py:28
  89.2 172.4 %reduce-scatter.3.cloned.1.call-start = ((), (), s32[]{:S(2)}) async-start(), calls=%async_computation.3 | async-start | bytes 6684672 | tf_op jit(solution)/shard_map/reduce_scatter | solution.py:31
  114.4 242.1 %copy-start.2 = (bf16[1,384,4096]{2,1,0:T(8,128)(2,1)S(1)}, bf16[1,384,4096]{2,1,0:T(8,128)(2,1)}, u32[]{:S(2)}) copy-start(bf16[1,384,4096]{2,1,0:T(8,128)(2,1)} %all-gather.11.cloned.1.call-done) | copy-start | bytes 9437188
  114.4 242.1 %copy-start.4 = (bf16[384,512]{1,0:T(8,128)(2,1)S(1)}, bf16[384,512]{1,0:T(8,128)(2,1)}, u32[]{:S(2)}) copy-start(bf16[384,512]{1,0:T(8,128)(2,1)} %all-reduce.5.cloned.1.call-done) | copy-start | bytes 1179652
  114.4 218.0 %all-gather.7.cloned.1.call-start = ((), (), s32[]{:S(2)}) async-start(), calls=%async_computation.4 | async-start | bytes 3342336 | tf_op jit(solution)/shard_map/all_gather | solution.py:49
  263.4 93.0 %all-reduce.7.cloned.1.call-start = ((), (), s32[]{:S(2)}) async-start(), calls=%async_computation.5 | async-start | bytes 786432 | tf_op jit(solution)/shard_map/psum | solution.py:56
  339.3 89.7 %all-gather.13.cloned.1.call-start = ((), (), s32[]{:S(2)}) async-start(), calls=%async_computation.11 | async-start | bytes 3342336 | tf_op jit(solution)/shard_map/all_gather | solution.py:17
  339.9 118.5 %all-reduce.9.cloned.1.call-start = ((), (), s32[]{:S(2)}) async-start(), calls=%async_computation.6 | async-start | bytes 786432 | tf_op jit(solution)/shard_map/psum | solution.py:28
  363.2 78.2 %copy-start.1 = (bf16[384,4096]{1,0:T(8,128)(2,1)S(1)}, bf16[384,4096]{1,0:T(8,128)(2,1)}, u32[]{:S(2)}) copy-start(bf16[384,4096]{1,0:T(8,128)(2,1)} %all-gather.7.cloned.1.call-done) | copy-start | bytes 9437188
  441.2 171.9 %reduce-scatter.5.cloned.1.call-start = ((), (), s32[]{:S(2)}) async-start(), calls=%async_computation.7 | async-start | bytes 6684672 | tf_op jit(solution)/shard_map/reduce_scatter | solution.py:31
  458.3 154.8 %copy-start.5 = (bf16[2,24,4096]{2,1,0:T(8,128)(2,1)S(1)}, bf16[2,24,4096]{2,1,0:T(8,128)(2,1)}, u32[]{:S(2)}) copy-start(bf16[2,24,4096]{2,1,0:T(8,128)(2,1)} %param.7) | copy-start | bytes 1179652
  466.4 224.6 %copy-start.3 = (bf16[384,512]{1,0:T(8,128)(2,1)S(1)}, bf16[384,512]{1,0:T(8,128)(2,1)}, u32[]{:S(2)}) copy-start(bf16[384,512]{1,0:T(8,128)(2,1)} %all-reduce.9.cloned.1.call-done) | copy-start | bytes 1179652
  466.5 217.7 %all-gather.9.cloned.1.call-start = ((), (), s32[]{:S(2)}) async-start(), calls=%async_computation.8 | async-start | bytes 3342336 | tf_op jit(solution)/shard_map/all_gather | solution.py:49
  614.9 93.3 %all-reduce.11.cloned.1.call-start = ((), (), s32[]{:S(2)}) async-start(), calls=%async_computation.9 | async-start | bytes 786432 | tf_op jit(solution)/shard_map/psum | solution.py:56
  691.1 17.1 %copy-start = (bf16[1,384,4096]{2,1,0:T(8,128)(2,1)S(1)}, bf16[1,384,4096]{2,1,0:T(8,128)(2,1)}, u32[]{:S(2)}) copy-start(bf16[1,384,4096]{2,1,0:T(8,128)(2,1)} %all-gather.13.cloned.1.call-done) | copy-start | bytes 9437188
Sparse Core Ops, SparseCore 0:
  11.3 70.8 all-gather.10
  89.3 16.9 all-reduce.4
  114.5 146.9 reduce-scatter.2
  265.1 67.2 all-gather.6
  339.4 16.9 all-reduce.6
  359.6 69.3 all-gather.12
  441.3 16.9 all-reduce.8
  466.6 146.4 reduce-scatter.4
  616.8 67.2 all-gather.8
  691.2 16.9 all-reduce.10
where the time goes:
time: 730 us; the launch traced here: 729 us
  waiting for transfers between devices  613 us (84%)
  matrix products  96 us (13%)
  between operations  14.2 us (2%)
    reduce_scatter x2, waiting for transfers between devices, local(): lax.psum_scatter(lax.dot_general(first_rows, second_half, (((1,), (1,)),...  294 us
    all_gather x2, waiting for transfers between devices, local(): lax.all_gather(inputs[round_index], 'replica', axis=0, tiled=True)  139 us
    all_gather x2, waiting for transfers between devices, local(): error_half = lax.all_gather(error_own, 'replica', axis=0, tiled=True)  138 us
    dot_general x2, matrix products, local(): lax.dot_general(error_half, first_rows, (((0,), (0,)), ((), ())), preferr...  25.9 us
    psum x2, waiting for transfers between devices, local(): lax.psum(first_terms.astype(jnp.bfloat16), 'dom').astype(jnp.float32)  22.8 us
    dot_general x2, matrix products, local(): lax.dot_general(first_error, round_batch, (((0,), (0,)), ((), ())), prefe...  21 us
    dot_general x2, matrix products, local(): lax.dot_general(round_batch, first_half, (((1,), (1,)), ((), ())), prefer...  19.1 us
    psum x2, waiting for transfers between devices, local(): lax.psum(back_terms.astype(jnp.bfloat16), 'dom').astype(jnp.float32)  18.9 us
  transfers between devices with their start and end apart: 10, of which 10 were waited for; matrix products, arithmetic and copies ran while one was open for 4% of the time, Pallas kernels for 0%

commit v1 on v0

--- a/solution.py
+++ b/solution.py
@@ -46,7 +46,16 @@
             * error_weight
             * (1.0 - second_out * second_out)
         ).astype(jnp.bfloat16)
-        error_half = lax.all_gather(error_own, "replica", axis=0, tiled=True)
+        block_now, far_arr = (jax.lax.axis_size("replica"), jax.lax.axis_index("replica"))
+        error_half, everything = (error_own, 1)
+        while everything < block_now:
+            even = jax.lax.ppermute(
+                error_half, "replica", tuple(((k, k ^ everything) for k in range(block_now)))
+            )
+            after = jnp.concatenate([error_half, even], axis=0)
+            spare = jnp.concatenate([even, error_half], axis=0)
+            error_half = jnp.where(far_arr & everything == 0, after, spare)
+            everything = 2 * everything
         second_grad = lax.dot_general(
             error_half, first_rows, (((0,), (0,)), ((), ())), preferred_element_type=jnp.float32
         )

time: 730 us -> 789 us (1.081)
  waiting for transfers between devices: 613 us -> 654 us
  starting transfers between devices: 0.59 us -> 10.1 us
    ppermute x0 -> x8, waiting for transfers between devices: none -> 184 us  [local(): jax.lax.ppermute(error_half, 'replica', tuple(((k, k ^ everything) for k...]
    all_gather x2 -> x0, waiting for transfers between devices: 138 us -> none  [local(): error_half = lax.all_gather(error_own, 'replica', axis=0, tiled=True)]
    ppermute x0 -> x8, starting transfers between devices: none -> 9.55 us  [local(): jax.lax.ppermute(error_half, 'replica', tuple(((k, k ^ everything) for k...]
  transfers between devices with their start and end apart: 10 -> 16, of which waited for: 10 -> 15; matrix products, arithmetic and copies ran while one was open for 4% -> 5% of each run, Pallas kernels for 0% -> 0%
where the time goes in v1:
time: 789 us
  waiting for transfers between devices  654 us (83%)
  matrix products  103 us (13%)
  between operations  14.2 us (2%)
  starting transfers between devices  10.1 us (1%)
    reduce_scatter x2, waiting for transfers between devices, local(): lax.psum_scatter(lax.dot_general(first_rows, second_half, (((1,), (1,)),...  294 us
    ppermute x8, waiting for transfers between devices, local(): jax.lax.ppermute(error_half, 'replica', tuple(((k, k ^ everything) for k...  184 us
    all_gather x2, waiting for transfers between devices, local(): lax.all_gather(inputs[round_index], 'replica', axis=0, tiled=True)  139 us
    dot_general x2, matrix products, local(): lax.dot_general(error_half, first_rows, (((0,), (0,)), ((), ())), preferr...  33.1 us
    dot_general x2, matrix products, local(): lax.dot_general(first_error, round_batch, (((0,), (0,)), ((), ())), prefe...  21 us
    psum x2, waiting for transfers between devices, local(): lax.psum(first_terms.astype(jnp.bfloat16), 'dom').astype(jnp.float32)  19.8 us
    dot_general x2, matrix products, local(): lax.dot_general(round_batch, first_half, (((1,), (1,)), ((), ())), prefer...  19.1 us
    psum x2, waiting for transfers between devices, local(): lax.psum(back_terms.astype(jnp.bfloat16), 'dom').astype(jnp.float32)  17.1 us
  transfers between devices with their start and end apart: 16, of which 15 were waited for; matrix products, arithmetic and copies ran while one was open for 5% of the time, Pallas kernels for 0%

profile of v1, /device:TPU:0, one launch (start us, length us, event | category | flops | bytes accessed | tf_op | source)
XLA Modules:
  0.0 789.0 jit_solution(5411567100600536380)
XLA Ops:
  9.1 73.1 %all-gather.5.cloned.1.call-done = bf16[1,384,4096]{2,1,0:T(8,128)(2,1)} async-done(((bf16[1,24,4096]{2,1,0:T(8,128)(2,1)}), bf16[1,384,4096]{2,1,0:T(8,128)(2,1)}) %all-gather.5.cloned.1.call-update) | async-done | bytes 3145744 | tf_op jit(solution)/shard_map/all_gather | solution.py:17
  82.2 6.9 fusion.37
  89.2 17.1 %all-reduce.5.cloned.1.call-done = bf16[384,512]{1,0:T(8,128)(2,1)} async-done(((bf16[384,512]{1,0:T(8,128)(2,1)}), bf16[384,512]{1,0:T(8,128)(2,1)}) %all-reduce.5.cloned.1.call-update) | async-done | bytes 393232 | tf_op jit(solution)/shard_map/psum | solution.py:28
  106.3 8.1 %convolution_multiply_fusion.1 = f32[384,4096]{1,0:T(8,128)} fusion(f32[4096,512]{1,0:T(8,128)} %param.10, bf16[384,512]{1,0:T(8,128)(2,1)} %all-reduce.5.cloned.1.call-done), kind=kOutput, calls=%fused_computation.9 | convolution fusion | flops 1614675968 | bytes 15073280 | tf_op jit(solution)/shard_map/dot_general | solution.py:32
  114.4 147.1 %reduce-scatter.3.cloned.1.call-done = f32[24,4096]{1,0:T(8,128)} async-done(((f32[384,4096]{1,0:T(8,128)}), f32[24,4096]{1,0:T(8,128)}) %reduce-scatter.3.cloned.1.call-update) | async-done | bytes 393232 | tf_op jit(solution)/shard_map/reduce_scatter | solution.py:31
  264.1 4.3 collective-permute-done
  270.0 7.0 collective-permute-done.1
  278.0 15.2 %collective-permute-done.2 = bf16[96,4096]{1,0:T(8,128)(2,1)S(1)} collective-permute-done((bf16[96,4096]{1,0:T(8,128)(2,1)S(1)}, bf16[96,4096]{1,0:T(8,128)(2,1)S(1)}, u32[]{:S(2)}, u32[]{:S(2)}) %collective-permute-start.2) | collective-permute-done | bytes 786464 | tf_op jit(solution)/shard_map/ppermute | solution.py:52
  295.4 65.6 %collective-permute-done.3 = bf16[192,4096]{1,0:T(8,128)(2,1)} collective-permute-done((bf16[192,4096]{1,0:T(8,128)(2,1)}, bf16[192,4096]{1,0:T(8,128)(2,1)}, u32[]{:S(2)}, u32[]{:S(2)}) %collective-permute-start.3) | collective-permute-done | bytes 1572896 | tf_op jit(solution)/shard_map/ppermute | solution.py:52
  361.0 7.8 fusion.45
  369.5 17.1 %all-reduce.7.cloned.1.call-done = bf16[384,512]{1,0:T(8,128)(2,1)} async-done(((bf16[384,512]{1,0:T(8,128)(2,1)}), bf16[384,512]{1,0:T(8,128)(2,1)}) %all-reduce.7.cloned.1.call-update) | async-done | bytes 393232 | tf_op jit(solution)/shard_map/psum | solution.py:65
  386.6 6.8 fusion.7
  393.4 65.8 %all-gather.7.cloned.1.call-done = bf16[1,384,4096]{2,1,0:T(8,128)(2,1)} async-done(((bf16[1,24,4096]{2,1,0:T(8,128)(2,1)}), bf16[1,384,4096]{2,1,0:T(8,128)(2,1)}) %all-gather.7.cloned.1.call-update) | async-done | bytes 3145744 | tf_op jit(solution)/shard_map/all_gather | solution.py:17
  459.2 12.2 %fusion.48 = bf16[384,512]{1,0:T(8,128)(2,1)} fusion(bf16[1,384,4096]{2,1,0:T(8,128)(2,1)} %all-gather.7.cloned.1.call-done, f32[512,4096]{1,0:T(8,128)} %param.8, f32[512,4096]{1,0:T(8,128)} %fusion.7, f32[512,4096]{1,0:T(8,128)} %param.9), kind=kOutput, calls=%fused_computation.38 | convolution fusion | flops 1623588864 | bytes 28704768 | tf_op jit(solution)/shard_map/dot_general | solution.py:20
  471.7 14.2 %multiply_subtract_fusion.2 = (f32[4096,512]{1,0:T(8,128)}, f32[4096,512]{1,0:T(8,128)}) fusion(f32[4096,512]{1,0:T(8,128)} %param.10, f32[4096,512]{1,0:T(8,128)} %param.11, bf16[384,512]{1,0:T(8,128)(2,1)S(1)} %copy-done.4, bf16[192,4096]{1,0:T(8,128)(2,1)} %collective-permute-done.3, bf16[192,4096]{1,0:T(8,128)(2,1)} %maximum_select_fusion.2, pred[]{:T(512)S(6)} %eq.16), kind=kOutput, calls=%fused_computation.4 | convolution fusion | flops 1635647488 | bytes 37093376 | tf_op jit(solution)/shard_map/dot_general | solution.py:59
  488.6 8.1 %convolution_multiply_fusion = f32[384,4096]{1,0:T(8,128)} fusion(f32[4096,512]{1,0:T(8,128)} %get-tuple-element.10, bf16[384,512]{1,0:T(8,128)(2,1)} %all-reduce.9.cloned.1.call-done), kind=kOutput, calls=%fused_computation.8 | convolution fusion | flops 1614675968 | bytes 15073280 | tf_op jit(solution)/shard_map/dot_general | solution.py:32
  496.7 146.6 %reduce-scatter.5.cloned.1.call-done = f32[24,4096]{1,0:T(8,128)} async-done(((f32[384,4096]{1,0:T(8,128)}), f32[24,4096]{1,0:T(8,128)}) %reduce-scatter.5.cloned.1.call-update) | async-done | bytes 393232 | tf_op jit(solution)/shard_map/reduce_scatter | solution.py:31
  645.9 4.2 collective-permute-done.4
  651.8 7.0 collective-permute-done.5
  659.9 16.0 %collective-permute-done.6 = bf16[96,4096]{1,0:T(8,128)(2,1)S(1)} collective-permute-done((bf16[96,4096]{1,0:T(8,128)(2,1)S(1)}, bf16[96,4096]{1,0:T(8,128)(2,1)S(1)}, u32[]{:S(2)}, u32[]{:S(2)}) %collective-permute-start.6) | collective-permute-done | bytes 786464 | tf_op jit(solution)/shard_map/ppermute | solution.py:52
  677.1 64.8 %collective-permute-done.7 = bf16[192,4096]{1,0:T(8,128)(2,1)S(1)} collective-permute-done((bf16[192,4096]{1,0:T(8,128)(2,1)S(1)}, bf16[192,4096]{1,0:T(8,128)(2,1)S(1)}, u32[]{:S(2)}, u32[]{:S(2)}) %collective-permute-start.7) | collective-permute-done | bytes 1572896 | tf_op jit(solution)/shard_map/ppermute | solution.py:52
  743.0 6.0 fusion.42
  749.1 18.8 %multiply_subtract_fusion = (f32[4096,512]{1,0:T(8,128)}, f32[4096,512]{1,0:T(8,128)}) fusion(f32[4096,512]{1,0:T(8,128)} %get-tuple-element.10, f32[4096,512]{1,0:T(8,128)} %param.11, f32[4096,512]{1,0:T(8,128)} %get-tuple-element.11, bf16[384,512]{1,0:T(8,128)(2,1)S(1)} %copy-done.3, bf16[192,4096]{1,0:T(8,128)(2,1)} %copy-done.5, ...), kind=kOutput, calls=%fused_computation | convolution fusion | flops 1639841792 | bytes 45481984 | tf_op jit(solution)/shard_map/dot_general | solution.py:59
  767.9 14.3 %multiply_subtract_fusion.1 = (f32[512,4096]{1,0:T(8,128)}, f32[512,4096]{1,0:T(8,128)}) fusion(f32[512,4096]{1,0:T(8,128)} %param.8, f32[512,4096]{1,0:T(8,128)} %param.9, f32[512,4096]{1,0:T(8,128)} %fusion.7, bf16[1,384,4096]{2,1,0:T(8,128)(2,1)S(1)} %copy-done, bf16[384,512]{1,0:T(8,128)(2,1)} %all-reduce.11.cloned.1.call-done, ...), kind=kOutput, calls=%fused_computation.2 | convolution fusion | flops 1632763904 | bytes 45875200 | tf_op jit(solution)/shard_map/dot_general | solution.py:67
  (51 shorter events, 20.8 us)
Async XLA Ops:
  7.2 75.1 %all-gather.5.cloned.1.call-start = ((), (), s32[]{:S(2)}) async-start(), calls=%async_computation.8 | async-start | bytes 3342336 | tf_op jit(solution)/shard_map/all_gather | solution.py:17
  9.0 97.3 %all-reduce.5.cloned.1.call-start = ((), (), s32[]{:S(2)}) async-start(), calls=%async_computation.2 | async-start | bytes 786432 | tf_op jit(solution)/shard_map/psum | solution.py:28
  89.2 172.4 %reduce-scatter.3.cloned.1.call-start = ((), (), s32[]{:S(2)}) async-start(), calls=%async_computation.3 | async-start | bytes 6684672 | tf_op jit(solution)/shard_map/reduce_scatter | solution.py:31
  114.4 147.2 %copy-start.6 = (bf16[2,24,4096]{2,1,0:T(8,128)(2,1)S(1)}, bf16[2,24,4096]{2,1,0:T(8,128)(2,1)}, u32[]{:S(2)}) copy-start(bf16[2,24,4096]{2,1,0:T(8,128)(2,1)} %param.7) | copy-start | bytes 1179652
  114.4 272.2 %all-reduce.7.cloned.1.call-start = ((), (), s32[]{:S(2)}) async-start(), calls=%async_computation.4 | async-start | bytes 786432 | tf_op jit(solution)/shard_map/psum | solution.py:65
  262.6 5.7 collective-permute-start
  268.4 8.5 %collective-permute-start.1 = (bf16[48,4096]{1,0:T(8,128)(2,1)S(1)}, bf16[48,4096]{1,0:T(8,128)(2,1)S(1)}, u32[]{:S(2)}, u32[]{:S(2)}) collective-permute-start(bf16[48,4096]{1,0:T(8,128)(2,1)S(1)} %maximum_select_fusion.10), channel_id=1, source_target_pairs={{0,4},{2,6},{4,0},{6,2},{8,12},{10,14},{12,8},{14,10},{16,20},{18,... | collective-permute-start | bytes 1179656 | tf_op jit(solution)/shard_map/ppermute | solution.py:52
  277.1 16.0 %collective-permute-start.2 = (bf16[96,4096]{1,0:T(8,128)(2,1)S(1)}, bf16[96,4096]{1,0:T(8,128)(2,1)S(1)}, u32[]{:S(2)}, u32[]{:S(2)}) collective-permute-start(bf16[96,4096]{1,0:T(8,128)(2,1)S(1)} %maximum_select_fusion.4), channel_id=1, source_target_pairs={{0,8},{2,10},{4,12},{6,14},{8,0},{10,2},{12,4},{14,6},{16,24},{18,... | collective-permute-start | bytes 2359304 | tf_op jit(solution)/shard_map/ppermute | solution.py:52
  294.6 66.4 %collective-permute-start.3 = (bf16[192,4096]{1,0:T(8,128)(2,1)}, bf16[192,4096]{1,0:T(8,128)(2,1)}, u32[]{:S(2)}, u32[]{:S(2)}) collective-permute-start(bf16[192,4096]{1,0:T(8,128)(2,1)} %maximum_select_fusion.2), channel_id=1, source_target_pairs={{0,16},{2,18},{4,20},{6,22},{8,24},{10,26},{12,28},{14,30},{16,0},... | collective-permute-start | bytes 4718600 | tf_op jit(solution)/shard_map/ppermute | solution.py:52
  295.4 91.2 %copy-start.1 = (bf16[1,384,4096]{2,1,0:T(8,128)(2,1)S(1)}, bf16[1,384,4096]{2,1,0:T(8,128)(2,1)}, u32[]{:S(2)}) copy-start(bf16[1,384,4096]{2,1,0:T(8,128)(2,1)} %all-gather.5.cloned.1.call-done) | copy-start | bytes 9437188
  295.4 91.2 %copy-start.4 = (bf16[384,512]{1,0:T(8,128)(2,1)S(1)}, bf16[384,512]{1,0:T(8,128)(2,1)}, u32[]{:S(2)}) copy-start(bf16[384,512]{1,0:T(8,128)(2,1)} %all-reduce.5.cloned.1.call-done) | copy-start | bytes 1179652
  368.9 90.3 %all-gather.7.cloned.1.call-start = ((), (), s32[]{:S(2)}) async-start(), calls=%async_computation.9 | async-start | bytes 3342336 | tf_op jit(solution)/shard_map/all_gather | solution.py:17
  369.5 119.1 %all-reduce.9.cloned.1.call-start = ((), (), s32[]{:S(2)}) async-start(), calls=%async_computation.5 | async-start | bytes 786432 | tf_op jit(solution)/shard_map/psum | solution.py:28
  471.4 171.9 %reduce-scatter.5.cloned.1.call-start = ((), (), s32[]{:S(2)}) async-start(), calls=%async_computation.6 | async-start | bytes 6684672 | tf_op jit(solution)/shard_map/reduce_scatter | solution.py:31
  496.6 146.7 %copy-start.7 = (bf16[2,24,4096]{2,1,0:T(8,128)(2,1)S(1)}, bf16[2,24,4096]{2,1,0:T(8,128)(2,1)}, u32[]{:S(2)}) copy-start(bf16[2,24,4096]{2,1,0:T(8,128)(2,1)} %param.7) | copy-start | bytes 1179652
  496.6 271.3 %all-reduce.11.cloned.1.call-start = ((), (), s32[]{:S(2)}) async-start(), calls=%async_computation.7 | async-start | bytes 786432 | tf_op jit(solution)/shard_map/psum | solution.py:65
  644.4 5.7 collective-permute-start.4
  650.2 8.5 %collective-permute-start.5 = (bf16[48,4096]{1,0:T(8,128)(2,1)S(1)}, bf16[48,4096]{1,0:T(8,128)(2,1)S(1)}, u32[]{:S(2)}, u32[]{:S(2)}) collective-permute-start(bf16[48,4096]{1,0:T(8,128)(2,1)S(1)} %maximum_select_fusion.11), channel_id=1, source_target_pairs={{0,4},{2,6},{4,0},{6,2},{8,12},{10,14},{12,8},{14,10},{16,20},{18,... | collective-permute-start | bytes 1179656 | tf_op jit(solution)/shard_map/ppermute | solution.py:52
  658.9 16.9 %collective-permute-start.6 = (bf16[96,4096]{1,0:T(8,128)(2,1)S(1)}, bf16[96,4096]{1,0:T(8,128)(2,1)S(1)}, u32[]{:S(2)}, u32[]{:S(2)}) collective-permute-start(bf16[96,4096]{1,0:T(8,128)(2,1)S(1)} %maximum_select_fusion.5), channel_id=1, source_target_pairs={{0,8},{2,10},{4,12},{6,14},{8,0},{10,2},{12,4},{14,6},{16,24},{18,... | collective-permute-start | bytes 2359304 | tf_op jit(solution)/shard_map/ppermute | solution.py:52
  676.2 65.7 %copy-start.2 = (bf16[192,4096]{1,0:T(8,128)(2,1)}, bf16[192,4096]{1,0:T(8,128)(2,1)S(1)}, u32[]{:S(2)}) copy-start(bf16[192,4096]{1,0:T(8,128)(2,1)S(1)} %maximum_select_fusion.3) | copy-start | bytes 4718596
  676.2 72.9 %copy-start.3 = (bf16[384,512]{1,0:T(8,128)(2,1)S(1)}, bf16[384,512]{1,0:T(8,128)(2,1)}, u32[]{:S(2)}) copy-start(bf16[384,512]{1,0:T(8,128)(2,1)} %all-reduce.9.cloned.1.call-done) | copy-start | bytes 1179652
  676.2 65.7 %collective-permute-start.7 = (bf16[192,4096]{1,0:T(8,128)(2,1)S(1)}, bf16[192,4096]{1,0:T(8,128)(2,1)S(1)}, u32[]{:S(2)}, u32[]{:S(2)}) collective-permute-start(bf16[192,4096]{1,0:T(8,128)(2,1)S(1)} %maximum_select_fusion.3), channel_id=1, source_target_pairs={{0,16},{2,18},{4,20},{6,22},{8,24},{10,26},{12,28},{14,30},{16,0},... | collective-permute-start | bytes 4718600 | tf_op jit(solution)/shard_map/ppermute | solution.py:52
  741.9 1.1 copy-start.5
  749.1 18.9 %copy-start = (bf16[1,384,4096]{2,1,0:T(8,128)(2,1)S(1)}, bf16[1,384,4096]{2,1,0:T(8,128)(2,1)}, u32[]{:S(2)}) copy-start(bf16[1,384,4096]{2,1,0:T(8,128)(2,1)} %all-gather.7.cloned.1.call-done) | copy-start | bytes 9437188
Sparse Core Ops, SparseCore 0:
  11.3 70.8 all-gather.4
  89.3 16.9 all-reduce.4
  114.5 146.9 reduce-scatter.2
  369.0 17.5 all-reduce.6
  389.8 69.3 all-gather.6
  471.6 16.9 all-reduce.8
  496.8 146.4 reduce-scatter.4
  749.2 17.5 all-reduce.10
